TPU v7x, 32 devices: a whole 2x2x4 slice. The times are simulated.
32 devices in a mesh: nodes: 16 (over z, y, x), stream: 2 (over core).
Axes of the slice: x: 2, y: 2, z: 4, core: 2. Of those that a mesh axis runs over, the one named last changes fastest.
Arguments:
- features: bfloat16 [5120, 1024], P('nodes'), may hold values from -6 to 6
- neighbours: int32 [5120, 50], P('nodes', 'stream'), may hold values from 0 to 5119, as said below
- present: int32 [5120, 50], P('nodes', 'stream'), may hold values from 0 to 1, as said below
- importance: int32 [5120, 50], P('nodes', 'stream'), may hold values from 1 to 64
- q_weight: bfloat16 [1024, 1024], replicated, may hold values from -0.1875 to 0.1875
- q_bias: float32 [1024], replicated, may hold values from -3 to 3
- w_weight: bfloat16 [2048, 1024], P('stream'), may hold values from -0.1875 to 0.1875
- w_bias: float32 [1024], replicated, may hold values from -3 to 3
- cotangent: bfloat16 [5120, 1024], P('nodes'), may hold values from -6 to 6
Outputs:
- embeddings: float32 [5120, 1024], P('nodes')
- feature_grad: float32 [5120, 1024], P('nodes', 'stream')
- q_weight_grad: float32 [1024, 1024], replicated
- q_bias_grad: float32 [1024], replicated
- w_weight_grad: float32 [2048, 1024], P('stream')
- w_bias_grad: float32 [1024], replicated
Inputs may be any that keep to these rules, and one draw needn't show every extreme that they name: `neighbours`: number a device's nodes' slots of one half of the 50 slots node by node, j = local node * 25 + slot within the half; slot j names a row of the block of 320 rows of device j % 16 of nodes, so that each device's block is named exactly 500 times by each device and half; a row may be named several times. Each node has between 5 and 50 present slots.
All inputs are finite; a program needn't handle non-finite values.
Results may differ from a plain program's by a relative error of at most 0.014.
The roundings to bfloat16 on the way count: a program that leaves them out, or rounds other values in their place, can miss the bound.
Values may be sent and summed in bfloat16 or wider, within the bound.
No kernel may reach another device: no remote copies, remote signals or barrier semaphores. Data moves between devices by JAX's collectives and lax.ppermute only.
A program may use at most 128 MiB of HBM per device.

v0:
```python
import jax
import jax.numpy as jnp
from jax import lax
from jax.sharding import PartitionSpec as P


def spread(value, axis, source):
    kept = jnp.where(lax.axis_index(axis) == source, value, 0).astype(value.dtype)
    return lax.psum(kept, axis)


def one_hot_rows(row_ids, count):
    return (row_ids[..., None] == jnp.arange(count, dtype=jnp.int32)).astype(jnp.bfloat16)


def on_device(
    features, neighbours, present, importance, q_weight, q_bias, w_weight, w_bias, cotangent
):
    node_rows, feature_dim = features.shape
    slot_count = neighbours.shape[1]
    owners_count = lax.axis_size("nodes")
    stream_index = lax.axis_index("stream")
    slot_total = node_rows * slot_count
    capacity = slot_total // owners_count
    local_row = neighbours.reshape(slot_total) % node_rows
    requests = local_row.reshape(capacity, owners_count).T
    shard_rows = lax.all_gather(features, "nodes", axis=0, tiled=True)
    shards = shard_rows.shape[0] // node_rows
    blocks_of = shard_rows.reshape(shards, node_rows, feature_dim)
    picked = jnp.einsum(
        "scr,srd->scd",
        one_hot_rows(requests, node_rows),
        blocks_of,
        preferred_element_type=jnp.float32,
    ).astype(jnp.bfloat16)
    slot_rows = jnp.transpose(picked, (1, 0, 2)).reshape(slot_total, feature_dim)
    weights = (present * importance).astype(jnp.float32)
    weight_half = jnp.sum(weights, axis=1)
    block_nodes = 32
    steps_count = node_rows // block_nodes
    row_blocks = slot_rows.reshape(steps_count, block_nodes * slot_count, feature_dim)
    weight_blocks = weights.reshape(steps_count, block_nodes, slot_count)

    def hidden_of(collected_rows):
        return jnp.dot(collected_rows, q_weight, preferred_element_type=jnp.float32) + q_bias

    def forward_block(inputs):
        collected_rows, importance_block_weights = inputs
        hidden_pre = hidden_of(collected_rows)
        hidden_state = jax.nn.relu(hidden_pre).reshape(block_nodes, slot_count, feature_dim)
        return jnp.einsum(
            "gk,gkd->gd", importance_block_weights, hidden_state, precision=lax.Precision.HIGHEST
        )

    weighted_numerator = lax.map(forward_block, (row_blocks, weight_blocks)).reshape(
        node_rows, feature_dim
    )
    weighted_numerator, weight_sum = lax.psum((weighted_numerator, weight_half), "stream")
    aggregate = (weighted_numerator / weight_sum[:, None]).astype(jnp.bfloat16)
    stream_input = jnp.where(stream_index == 0, features, aggregate)
    partial_value = jnp.dot(stream_input, w_weight, preferred_element_type=jnp.float32)
    linear = lax.psum(partial_value, "stream") + w_bias
    relu_out = jax.nn.relu(linear)
    norm_scale = lax.rsqrt(jnp.mean(relu_out * relu_out, axis=1, keepdims=True) + 1e-06)
    embeddings = relu_out * norm_scale
    grad_out = cotangent.astype(jnp.float32)
    grad_relu = norm_scale * grad_out - relu_out * (
        norm_scale * norm_scale * norm_scale
    ) * jnp.mean(relu_out * grad_out, axis=1, keepdims=True)
    grad_linear = jnp.where(linear > 0, grad_relu, 0.0).astype(jnp.bfloat16)
    w_grad_local = lax.dot_general(
        stream_input, grad_linear, (((0,), (0,)), ((), ())), preferred_element_type=jnp.float32
    )
    w_bias_local = jnp.sum(grad_linear.astype(jnp.float32), axis=0)
    back_rows = lax.dot_general(
        grad_linear, w_weight, (((1,), (1,)), ((), ())), preferred_element_type=jnp.float32
    )
    grad_aggregate = spread(back_rows, "stream", 1)
    self_grad = jnp.where(stream_index == 0, back_rows, 0.0)
    grad_sum = grad_aggregate / weight_sum[:, None]
    grad_blocks = grad_sum.reshape(steps_count, block_nodes, feature_dim)

    def backward_block(totals, inputs):
        q_total, bias_total = totals
        collected_rows, importance_block_weights, grad_block = inputs
        hidden_pre = hidden_of(collected_rows)
        grad_hidden = (importance_block_weights[:, :, None] * grad_block[:, None, :]).reshape(
            block_nodes * slot_count, feature_dim
        )
        grad_hidden = jnp.where(hidden_pre > 0, grad_hidden, 0.0).astype(jnp.bfloat16)
        q_total = q_total + lax.dot_general(
            collected_rows,
            grad_hidden,
            (((0,), (0,)), ((), ())),
            preferred_element_type=jnp.float32,
        )
        bias_total = bias_total + jnp.sum(grad_hidden.astype(jnp.float32), axis=0)
        grad_rows = lax.dot_general(
            grad_hidden, q_weight, (((1,), (1,)), ((), ())), preferred_element_type=jnp.float32
        ).astype(jnp.bfloat16)
        return ((q_total, bias_total), grad_rows)

    start_totals = (
        jnp.zeros((feature_dim, feature_dim), jnp.float32),
        jnp.zeros((feature_dim,), jnp.float32),
    )
    (q_grad_local, q_bias_local), grad_rows = lax.scan(
        backward_block, start_totals, (row_blocks, weight_blocks, grad_blocks)
    )
    grad_buffer = jnp.transpose(grad_rows.reshape(capacity, owners_count, feature_dim), (1, 0, 2))
    asked_rows, returned = (
        lax.all_to_all(requests, "nodes", split_axis=0, concat_axis=0, tiled=True),
        lax.all_to_all(grad_buffer, "nodes", split_axis=0, concat_axis=0, tiled=True),
    )
    neighbour_grad = lax.dot_general(
        one_hot_rows(asked_rows.reshape(-1), node_rows),
        returned.reshape(-1, feature_dim),
        (((0,), (0,)), ((), ())),
        preferred_element_type=jnp.float32,
    )
    feature_grad = lax.psum_scatter(
        self_grad + neighbour_grad, "stream", scatter_dimension=1, tiled=True
    )
    w_grad, w_bias_grad, q_grad, q_bias_grad = lax.psum(
        (w_grad_local, w_bias_local, q_grad_local, q_bias_local), "nodes"
    )
    q_grad, q_bias_grad = lax.psum((q_grad, q_bias_grad), "stream")
    return (embeddings, feature_grad, q_grad, q_bias_grad, w_grad, w_bias_grad)


def solution(mesh):
    in_specs = (
        P("nodes", None),
        P("nodes", "stream"),
        P("nodes", "stream"),
        P("nodes", "stream"),
        P(),
        P(),
        P("stream", None),
        P(),
        P("nodes", None),
    )
    out_specs = (P("nodes", None), P("nodes", "stream"), P(), P(), P("stream", None), P())
    return jax.shard_map(
        on_device, mesh=mesh, in_specs=in_specs, out_specs=out_specs, check_vma=False
    )
```

profile of v0, /device:TPU:0, one launch (start us, length us, event | category | flops | bytes accessed | tf_op | source)
XLA Modules:
  0.0 1334.9 jit_solution(5990324770737478218)
XLA Ops:
  10.2 135.5 %all-gather.2.cloned.1.call-done = bf16[5120,1024]{1,0:T(8,128)(2,1)} async-done(((bf16[320,1024]{1,0:T(8,128)(2,1)}), bf16[5120,1024]{1,0:T(8,128)(2,1)}) %all-gather.2.cloned.1.call-update) | async-done | bytes 10485776 | tf_op jit(solution)/shard_map/all_gather | solution.py:27
  145.7 16.2 %convert_bitcast_fusion = bf16[500,16,1024]{2,0,1:T(8,128)(2,1)} fusion(bf16[16,320,1024]{2,1,0:T(8,128)(2,1)} %bitcast.85, s32[16,500]{1,0:T(8,128)S(1)} %copy.35), kind=kOutput, calls=%fused_computation.22 | convolution fusion | flops 5253632000 | bytes 26901760 | tf_op jit(solution)/shard_map/scr,srd->scd/dot_general | solution.py:30
  161.9 15.5 %copy.36 = bf16[500,16,1024]{2,1,0:T(8,128)(2,1)} copy(bf16[500,16,1024]{2,0,1:T(8,128)(2,1)} %convert_bitcast_fusion) | data formatting | bytes 32768000 | tf_op jit(solution)/shard_map/convert_element_type | solution.py:35
  177.4 143.1 %while.25 = (s32[]{:T(128)}, f32[10,32,1024]{2,1,0:T(8,128)}, f32[10,32,25]{2,1,0:T(8,128)S(1)}, bf16[10,800,1024]{2,1,0:T(8,128)(2,1)}, bf16[1024,1024]{1,0:T(8,128)(2,1)}, /*index=5*/f32[1024]{0:T(1024)S(1)}, s32[]{:T(128)}) while((s32[]{:T(128)}, f32[10,32,1024]{2,1,0:T(8,128)}, f32[10,32,25]{2,1,0:T(8,128)S(1)}, ...), condition=%wide.region_1.2_spmd, body=%wide.region_0.1_spmd.sunk | while | flops 1689190400 | bytes 17250768 | solution.py:55
  177.4 5.7 add_maximum_fusion.3
  183.2 3.7 reshape.83
  186.8 4.3 fusion.56
  191.8 5.7 add_maximum_fusion.3
  197.5 3.7 reshape.83
  201.1 4.3 fusion.56
  206.1 5.7 add_maximum_fusion.3
  211.8 3.7 reshape.83
  215.4 4.3 fusion.56
  220.4 5.7 add_maximum_fusion.3
  226.0 3.7 reshape.83
  229.7 4.3 fusion.56
  234.7 5.7 add_maximum_fusion.3
  240.3 3.7 reshape.83
  244.0 4.3 fusion.56
  249.0 5.7 add_maximum_fusion.3
  254.6 3.7 reshape.83
  258.3 4.3 fusion.56
  263.3 5.7 add_maximum_fusion.3
  272.6 4.3 fusion.56
  277.6 5.7 add_maximum_fusion.3
  283.2 3.7 reshape.83
  286.9 4.3 fusion.56
  291.9 5.7 add_maximum_fusion.3
  301.2 4.3 fusion.56
  306.2 5.7 add_maximum_fusion.3
  311.8 3.7 reshape.83
  315.5 4.3 fusion.56
  323.0 15.8 %all-reduce.8.cloned.1.call-done = f32[320,1024]{1,0:T(8,128)} async-done(((f32[320,1024]{1,0:T(8,128)}), f32[320,1024]{1,0:T(8,128)}) %all-reduce.8.cloned.1.call-update) | async-done | bytes 1310736 | tf_op jit(solution)/shard_map/psum | solution.py:58
  342.7 21.1 %all-reduce.10.cloned.1.call-done = f32[320,1024]{1,0:T(8,128)} async-done(((f32[320,1024]{1,0:T(8,128)}), f32[320,1024]{1,0:T(8,128)}) %all-reduce.10.cloned.1.call-update) | async-done | bytes 1310736 | tf_op jit(solution)/shard_map/psum | solution.py:62
  371.3 6.8 all-to-all-start
  378.1 12.8 all-reduce.12.cloned.1.call-done
  392.5 239.1 %while.26 = (s32[]{:T(128)}, f32[1024,1024]{1,0:T(8,128)}, f32[1024]{0:T(1024)S(1)}, bf16[10,800,1024]{2,1,0:T(8,128)(2,1)}, bf16[10,800,1024]{2,1,0:T(8,128)(2,...) while((s32[]{:T(128)}, f32[1024,1024]{1,0:T(8,128)}, ...), condition=%wide.region_11.12_spmd.clone, body=%wide.region_9.11_spmd.clone.sunk | while | flops 5041816576 | bytes 50894132 | solution.py:107
  399.4 5.2 convert_reduce_fusion.3
  408.9 6.3 select_add_fusion.4
  422.2 5.2 convert_reduce_fusion.3
  431.7 7.6 select_add_fusion.4
  446.2 5.2 convert_reduce_fusion.3
  455.7 7.6 select_add_fusion.4
  470.3 5.2 convert_reduce_fusion.3
  479.7 7.6 select_add_fusion.4
  494.3 5.2 convert_reduce_fusion.3
  503.7 7.6 select_add_fusion.4
  518.3 5.2 convert_reduce_fusion.3
  527.8 7.6 select_add_fusion.4
  542.4 5.2 convert_reduce_fusion.3
  551.9 7.6 select_add_fusion.4
  566.4 5.2 convert_reduce_fusion.3
  575.9 7.6 select_add_fusion.4
  590.4 5.2 convert_reduce_fusion.3
  599.9 7.6 select_add_fusion.4
  614.5 5.2 convert_reduce_fusion.3
  624.0 7.6 select_add_fusion.4
  631.6 15.5 %copy.43 = bf16[500,16,1024]{2,0,1:T(8,128)(2,1)} copy(bf16[500,16,1024]{2,1,0:T(8,128)(2,1)} %bitcast.14) | data formatting | bytes 32768000 | tf_op jit(solution)/shard_map/reshape | solution.py:110
  647.1 6.8 all-to-all-start.1
  657.3 592.5 %all-reduce.16.cloned.1.call-done = (f32[1024,1024]{1,0:T(8,128)}, f32[1024,1024]{1,0:T(8,128)}) async-done(((f32[1024,1024]{1,0:T(8,128)}, f32[1024,1024]{1,0:T(8,128)}), (f32[1024,1024]{1,0:T(8,128)}, f32[1024,1024]{1,0:T(8,128)})) %all-reduce.16.cloned.1.call-update) | async-done | bytes 8388624 | tf_op jit(solution)/shard_map/psum | solution.py:124
  1250.3 15.0 %reshape.78 = bf16[8000,1024]{1,0:T(8,128)(2,1)} reshape(bf16[16,500,1024]{2,1,0:T(8,128)(2,1)} %all-to-all-done.1) | data formatting | bytes 32768000 | tf_op jit(solution)/shard_map/reshape | solution.py:117
  1265.3 10.4 fusion.13
  1275.7 41.2 %all-reduce = (f32[1024]{0:T(1024)S(1)}, f32[1024]{0:T(1024)}) all-reduce(f32[1024]{0:T(1024)S(1)} %get-tuple-element.90, f32[1024]{0:T(1024)S(1)} %get-tuple-element.157), channel_id=1, replica_groups=mesh['nodes'=16,'stream'=2] {'nodes'}, use_global_device_ids=true, to_apply=%region_15.16 | all-reduce | flops 2048 | bytes 16384 | tf_op jit(solution)/shard_map/psum | solution.py:124
  1320.0 4.9 copy.72
  (201 shorter events, 154.5 us)
Async XLA Ops:
  7.2 333.3 %copy-start = (bf16[1024,1024]{1,0:T(8,128)(2,1)S(1)}, bf16[1024,1024]{1,0:T(8,128)(2,1)}, u32[]{:S(2)}) copy-start(bf16[1024,1024]{1,0:T(8,128)(2,1)} %param.19) | copy-start | bytes 6291460
  7.2 2.8 copy-start.9
  7.2 2.8 copy-start.10
  7.2 138.5 %all-gather.2.cloned.1.call-start = ((), (), s32[]{:S(2)}) async-start(), calls=%async_computation.3 | async-start | bytes 11141120 | tf_op jit(solution)/shard_map/all_gather | solution.py:27
  7.9 330.9 %all-reduce.8.cloned.1.call-start = ((), (), s32[]{:S(2)}) async-start(), calls=%async_computation.4 | async-start | bytes 2621440 | tf_op jit(solution)/shard_map/psum | solution.py:58
  161.9 15.5 %copy-start.13 = (f32[1024]{0:T(1024)S(1)}, f32[1024]{0:T(1024)}, u32[]{:S(2)}) copy-start(f32[1024]{0:T(1024)} %param.18) | copy-start | bytes 12292
  177.4 161.4 %copy-start.4 = (bf16[320,1024]{1,0:T(8,128)(2,1)S(1)}, bf16[320,1024]{1,0:T(8,128)(2,1)}, u32[]{:S(2)}) copy-start(bf16[320,1024]{1,0:T(8,128)(2,1)} %param.13) | copy-start | bytes 1966084
  320.5 2.6 copy-start.8
  320.5 43.2 %all-reduce.10.cloned.1.call-start = ((), (), s32[]{:S(2)}) async-start(), calls=%async_computation.5 | async-start | bytes 2621440 | tf_op jit(solution)/shard_map/psum | solution.py:62
  340.5 23.3 %copy-start.5 = (bf16[320,1024]{1,0:T(8,128)(2,1)S(1)}, bf16[320,1024]{1,0:T(8,128)(2,1)}, u32[]{:S(2)}) copy-start(bf16[320,1024]{1,0:T(8,128)(2,1)} %param.21) | copy-start | bytes 1966084
  340.5 23.3 %copy-start.11 = (f32[1024]{0:T(1024)S(1)}, f32[1024]{0:T(1024)}, u32[]{:S(2)}) copy-start(f32[1024]{0:T(1024)} %param.20) | copy-start | bytes 12292
  342.4 48.5 %all-reduce.12.cloned.1.call-start = ((), (), s32[]{:S(2)}) async-start(), calls=%async_computation.6 | async-start | bytes 2621440 | tf_op jit(solution)/shard_map/psum | solution.py:9
  363.8 1.9 copy-start.2
  363.8 1.9 copy-start.6
  371.3 275.8 %all-to-all-start = ((s32[16,1,500]{2,1,0:T(1,128)}), s32[16,1,500]{2,1,0:T(1,128)S(1)}, u32[]{:S(2)}, u32[]{:S(2)}) async-start(s32[16,1,500]{2,1,0:T(1,128)} %copy.37), calls=%async_computation | async-start | bytes 65536 | tf_op jit(solution)/shard_map/all_to_all | solution.py:112
  399.4 6.4 copy-start.12
  404.7 1.2 copy-start.14
  422.2 6.4 copy-start.12
  427.4 1.2 copy-start.14
  446.2 6.4 copy-start.12
  451.4 1.2 copy-start.14
  470.3 6.4 copy-start.12
  475.5 1.2 copy-start.14
  494.3 6.4 copy-start.12
  499.5 1.2 copy-start.14
  518.3 6.4 copy-start.12
  523.5 1.2 copy-start.14
  542.4 6.4 copy-start.12
  547.6 1.2 copy-start.14
  566.4 6.4 copy-start.12
  571.7 1.2 copy-start.14
  590.4 6.4 copy-start.12
  595.7 1.2 copy-start.14
  614.5 6.4 copy-start.12
  619.7 1.2 copy-start.14
  647.1 603.3 %all-to-all-start.1 = ((bf16[16,500,1024]{2,1,0:T(8,128)(2,1)}), bf16[16,500,1024]{2,1,0:T(8,128)(2,1)}, u32[]{:S(2)}, u32[]{:S(2)}) async-start(bf16[16,500,1024]{2,1,0:T(8,128)(2,1)} %bitcast.80), calls=%async_computation.1 | async-start | bytes 33030144 | tf_op jit(solution)/shard_map/all_to_all | solution.py:113
  653.9 595.9 %all-reduce.16.cloned.1.call-start = ((), (), s32[]{:S(2)}) async-start(), calls=%async_computation.9 | async-start | bytes 16777216 | tf_op jit(solution)/shard_map/psum | solution.py:124
  657.3 662.7 %all-reduce.14.cloned.1.call-start = ((), (), s32[]{:S(2)}) async-start(), calls=%async_computation.8 | async-start | bytes 8388608 | tf_op jit(solution)/shard_map/psum | solution.py:127
  1249.9 70.1 %reduce-scatter.2.cloned.1.call-start = ((), (), s32[]{:S(2)}) async-start(), calls=%async_computation.7 | async-start | bytes 1966080 | tf_op jit(solution)/shard_map/reduce_scatter | solution.py:121
  1250.3 15.0 %copy-start.7 = (f32[320,1024]{1,0:T(8,128)S(1)}, f32[320,1024]{1,0:T(8,128)}, u32[]{:S(2)}) copy-start(f32[320,1024]{1,0:T(8,128)} %get-tuple-element.169) | copy-start | bytes 3932164
  1320.0 4.9 copy-start.3
  1324.9 3.1 copy-start.1
Sparse Core Ops, SparseCore 0:
  10.7 134.8 all-gather.1
  320.6 18.1 all-reduce.7
  342.5 21.1 all-reduce.9
  369.8 21.1 all-reduce.11
  662.3 587.4 all-reduce.15
  1252.3 27.3 all-reduce.13
  1282.6 9.9 reduce-scatter.1
where the time goes:
time: 1340 us; the launch traced here: 1330 us
  waiting for transfers between devices  779 us (58%)
  matrix products  291 us (22%)
  local copies, waits for them, and re-layouts  181 us (14%)
  blocking collectives  46.7 us (3%)
  starting transfers between devices  14.3 us (1%)
  between operations  14.3 us (1%)
    psum x1, waiting for transfers between devices, on_device(): lax.psum((w_grad_local, w_bias_local, q_grad_local, q_bias_local), 'nodes')  593 us
    all_gather x1, waiting for transfers between devices, on_device(): shard_rows = lax.all_gather(features, 'nodes', axis=0, tiled=True)  135 us
    dot_general x20, matrix products, hidden_of(): jnp.dot(collected_rows, q_weight, preferred_element_type=jnp.float32)  109 us
    dot_general x10, matrix products, backward_block(): lax.dot_general(collected_rows, grad_hidden, (((0,), (0,)), ((), ())), pr...  74.6 us
    mul x40, local copies, waits for them, and re-layouts, backward_block(): importance_block_weights[:, :, None] * grad_block[:, None, :]  62.3 us
    dot_general x10, matrix products, forward_block(): jnp.einsum('gk,gkd->gd', importance_block_weights, hidden_state, precisio...  42.9 us
    psum x1, blocking collectives, on_device(): lax.psum((w_grad_local, w_bias_local, q_grad_local, q_bias_local), 'nodes')  41.2 us
    reshape x10, local copies, waits for them, and re-layouts, forward_block(): jax.nn.relu(hidden_pre).reshape(block_nodes, slot_count, feature_dim)  36.6 us
  transfers between devices with their start and end apart: 9, of which 5 were waited for; matrix products, arithmetic and copies ran while one was open for 21% of the time, Pallas kernels for 0%

commit v1 on v0

--- a/solution.py
+++ b/solution.py
@@ -2,6 +2,33 @@
 import jax.numpy as jnp
 from jax import lax
 from jax.sharding import PartitionSpec as P
+
+
+def lines_report(slab_in, mesh_dim, d_out):
+    h_now, carry_out, r1 = (
+        jax.lax.axis_size(mesh_dim),
+        jax.lax.axis_index(mesh_dim),
+        slab_in.shape[d_out],
+    )
+    blocks_here = tuple(((ix, (ix + 1) % h_now) for ix in range(h_now)))
+    ledger = tuple(((ix, (ix - 1) % h_now) for ix in range(h_now)))
+    t_next = jnp.zeros(
+        (*slab_in.shape[:d_out], h_now * r1, *slab_in.shape[d_out + 1 :]), slab_in.dtype
+    )
+    t_next = lax.dynamic_update_slice_in_dim(t_next, slab_in, carry_out * r1, axis=d_out)
+    block_now = low = slab_in
+    b_now = h_now // 2
+    for i in [*range(1, b_now + 1)]:
+        block_now = jax.lax.ppermute(block_now, mesh_dim, blocks_here)
+        t_next = lax.dynamic_update_slice_in_dim(
+            t_next, block_now, (carry_out - i) % h_now * r1, axis=d_out
+        )
+        if i < h_now - b_now:
+            low = jax.lax.ppermute(low, mesh_dim, ledger)
+            t_next = lax.dynamic_update_slice_in_dim(
+                t_next, low, (carry_out + i) % h_now * r1, axis=d_out
+            )
+    return t_next
 
 
 def spread(value, axis, source):
@@ -24,7 +51,7 @@
     capacity = slot_total // owners_count
     local_row = neighbours.reshape(slot_total) % node_rows
     requests = local_row.reshape(capacity, owners_count).T
-    shard_rows = lax.all_gather(features, "nodes", axis=0, tiled=True)
+    shard_rows = lines_report(features, "nodes", d_out=0)
     shards = shard_rows.shape[0] // node_rows
     blocks_of = shard_rows.reshape(shards, node_rows, feature_dim)
     picked = jnp.einsum(

time: 1340 us -> 1450 us (1.082)
  starting transfers between devices: 14.3 us -> 118 us
  local copies, waits for them, and re-layouts: 181 us -> 214 us
  waiting for transfers between devices: 779 us -> 749 us
    all_gather x1 -> x0, waiting for transfers between devices: 135 us -> none  [on_device(): shard_rows = lax.all_gather(features, 'nodes', axis=0, tiled=True)]
    ppermute x0 -> x15, starting transfers between devices: none -> 104 us  [the longest x7 90.6 us: lines_report(): low = jax.lax.ppermute(low, mesh_dim, ledger)]
    ppermute x0 -> x15, waiting for transfers between devices: none -> 99.4 us  [the longest x8 88.4 us: lines_report(): block_now = jax.lax.ppermute(block_now, mesh_dim, blocks_here)]
    dynamic_update_slice x0 -> x16, local copies, waits for them, and re-layouts: none -> 20.8 us  [the longest x8 10.4 us: lines_report(): lax.dynamic_update_slice_in_dim(t_next, block_now, (carry_out - i) % h_no...]
  transfers between devices with their start and end apart: 9 -> 23, of which waited for: 5 -> 12; matrix products, arithmetic and copies ran while one was open for 21% -> 21% of each run, Pallas kernels for 0% -> 0%
where the time goes in v1:
time: 1450 us; the launch traced here: 1440 us
  waiting for transfers between devices  749 us (52%)
  matrix products  291 us (20%)
  local copies, waits for them, and re-layouts  214 us (15%)
  starting transfers between devices  118 us (8%)
  blocking collectives  46.8 us (3%)
    psum x1, waiting for transfers between devices, on_device(): lax.psum((w_grad_local, w_bias_local, q_grad_local, q_bias_local), 'nodes')  592 us
    dot_general x20, matrix products, hidden_of(): jnp.dot(collected_rows, q_weight, preferred_element_type=jnp.float32)  109 us
    ppermute x7, starting transfers between devices, lines_report(): low = jax.lax.ppermute(low, mesh_dim, ledger)  90.6 us
    ppermute x8, waiting for transfers between devices, lines_report(): block_now = jax.lax.ppermute(block_now, mesh_dim, blocks_here)  88.4 us
    dot_general x10, matrix products, backward_block(): lax.dot_general(collected_rows, grad_hidden, (((0,), (0,)), ((), ())), pr...  74.6 us
    mul x40, local copies, waits for them, and re-layouts, backward_block(): importance_block_weights[:, :, None] * grad_block[:, None, :]  62.7 us
    dot_general x10, matrix products, forward_block(): jnp.einsum('gk,gkd->gd', importance_block_weights, hidden_state, precisio...  42.9 us
    psum x1, blocking collectives, on_device(): lax.psum((w_grad_local, w_bias_local, q_grad_local, q_bias_local), 'nodes')  41.3 us
  transfers between devices with their start and end apart: 23, of which 12 were waited for; matrix products, arithmetic and copies ran while one was open for 21% of the time, Pallas kernels for 0%

profile of v1, /device:TPU:0, one launch (start us, length us, event | category | flops | bytes accessed | tf_op | source)
XLA Modules:
  0.0 1444.3 jit_solution(4662037514169532764)
XLA Ops:
  14.3 24.3 %collective-permute-done = bf16[320,1024]{1,0:T(8,128)(2,1)S(1)} collective-permute-done((bf16[320,1024]{1,0:T(8,128)(2,1)}, bf16[320,1024]{1,0:T(8,128)(2,1)S(1)}, u32[]{:S(2)}, u32[]{:S(2)}) %collective-permute-start) | collective-permute-done | bytes 655392 | tf_op jit(solution)/shard_map/ppermute | solution.py:22
  44.2 23.9 %collective-permute-done.2 = bf16[320,1024]{1,0:T(8,128)(2,1)S(1)} collective-permute-done((bf16[320,1024]{1,0:T(8,128)(2,1)S(1)}, bf16[320,1024]{1,0:T(8,128)(2,1)S(1)}, u32[]{:S(2)}, u32[]{:S(2)}) %collective-permute-start.2) | collective-permute-done | bytes 655392 | tf_op jit(solution)/shard_map/ppermute | solution.py:22
  73.7 23.1 %collective-permute-done.4 = bf16[320,1024]{1,0:T(8,128)(2,1)S(1)} collective-permute-done((bf16[320,1024]{1,0:T(8,128)(2,1)S(1)}, bf16[320,1024]{1,0:T(8,128)(2,1)S(1)}, u32[]{:S(2)}, u32[]{:S(2)}) %collective-permute-start.4) | collective-permute-done | bytes 655392 | tf_op jit(solution)/shard_map/ppermute | solution.py:22
  99.3 16.0 %collective-permute-start.7 = (bf16[320,1024]{1,0:T(8,128)(2,1)}, bf16[320,1024]{1,0:T(8,128)(2,1)}, u32[]{:S(2)}, u32[]{:S(2)}) collective-permute-start(bf16[320,1024]{1,0:T(8,128)(2,1)} %collective-permute-done.5), channel_id=1, source_target_pairs={{0,30},{2,0},{4,2},{6,4},{8,6},{10,8},{12,10},{14,12},{16,14},{18,... | collective-permute-start | bytes 1966088 | tf_op jit(solution)/shard_map/ppermute | solution.py:27
  115.3 10.2 collective-permute-done.6
  129.3 31.2 %collective-permute-start.9 = (bf16[320,1024]{1,0:T(8,128)(2,1)}, bf16[320,1024]{1,0:T(8,128)(2,1)}, u32[]{:S(2)}, u32[]{:S(2)}) collective-permute-start(bf16[320,1024]{1,0:T(8,128)(2,1)} %collective-permute-done.7), channel_id=1, source_target_pairs={{0,30},{2,0},{4,2},{6,4},{8,6},{10,8},{12,10},{14,12},{16,14},{18,... | collective-permute-start | bytes 1966088 | tf_op jit(solution)/shard_map/ppermute | solution.py:27
  162.9 5.3 broadcast_in_dim.27
  174.1 16.5 %collective-permute-start.11 = (bf16[320,1024]{1,0:T(8,128)(2,1)}, bf16[320,1024]{1,0:T(8,128)(2,1)S(1)}, u32[]{:S(2)}, u32[]{:S(2)}) collective-permute-start(bf16[320,1024]{1,0:T(8,128)(2,1)} %collective-permute-done.9), channel_id=1, source_target_pairs={{0,30},{2,0},{4,2},{6,4},{8,6},{10,8},{12,10},{14,12},{16,14},{18,... | collective-permute-start | bytes 1966088 | tf_op jit(solution)/shard_map/ppermute | solution.py:27
  198.2 5.1 collective-permute-done.11
  203.3 16.5 %collective-permute-start.13 = (bf16[320,1024]{1,0:T(8,128)(2,1)S(1)}, bf16[320,1024]{1,0:T(8,128)(2,1)S(1)}, u32[]{:S(2)}, u32[]{:S(2)}) collective-permute-start(bf16[320,1024]{1,0:T(8,128)(2,1)S(1)} %collective-permute-done.11), channel_id=1, source_target_pairs={{0,30},{2,0},{4,2},{6,4},{8,6},{10,8},{12,10},{14,12},{16,14},{18,... | collective-permute-start | bytes 1966088 | tf_op jit(solution)/shard_map/ppermute | solution.py:27
  232.2 6.9 collective-permute-done.14
  240.0 16.3 %convert_bitcast_fusion = bf16[500,16,1024]{2,0,1:T(8,128)(2,1)} fusion(bf16[16,320,1024]{2,1,0:T(8,128)(2,1)} %bitcast.8, s32[16,500]{1,0:T(8,128)S(1)} %copy.35), kind=kOutput, calls=%fused_computation.22 | convolution fusion | flops 5253632000 | bytes 26901760 | tf_op jit(solution)/shard_map/scr,srd->scd/dot_general | solution.py:57
  256.3 15.5 %copy.36 = bf16[500,16,1024]{2,1,0:T(8,128)(2,1)} copy(bf16[500,16,1024]{2,0,1:T(8,128)(2,1)} %convert_bitcast_fusion) | data formatting | bytes 32768000 | tf_op jit(solution)/shard_map/convert_element_type | solution.py:62
  271.8 150.1 %while.25 = (s32[]{:T(128)}, f32[10,32,1024]{2,1,0:T(8,128)}, f32[10,32,25]{2,1,0:T(8,128)}, bf16[10,800,1024]{2,1,0:T(8,128)(2,1)}, bf16[1024,1024]{1,0:T(8,128)(2,1)}, /*index=5*/f32[1024]{0:T(1024)S(1)}, s32[]{:T(128)}) while((s32[]{:T(128)}, f32[10,32,1024]{2,1,0:T(8,128)}, f32[10,32,25]{2,1,0:T(8,128)}, bf16[10,800,1024]{2,1,0:T(8,128)(2,1)}, ...), condition=%wide.region_1.2_spmd, body=%wide.region_0.1_spmd.sunk | while | flops 1689190400 | bytes 17250768 | solution.py:82
  271.8 5.7 add_maximum_fusion.3
  281.9 4.3 fusion.56
  286.9 5.7 add_maximum_fusion.3
  296.9 4.3 fusion.56
  301.9 5.7 add_maximum_fusion.3
  311.9 4.3 fusion.56
  316.9 5.7 add_maximum_fusion.3
  331.9 5.7 add_maximum_fusion.3
  341.9 4.3 fusion.56
  346.9 5.7 add_maximum_fusion.3
  357.0 4.3 fusion.56
  361.9 5.7 add_maximum_fusion.3
  372.0 4.3 fusion.56
  376.9 5.7 add_maximum_fusion.3
  387.0 4.3 fusion.56
  392.0 5.7 add_maximum_fusion.3
  402.0 4.3 fusion.56
  407.0 5.7 add_maximum_fusion.3
  424.5 22.8 %all-reduce.8.cloned.1.call-done = f32[320,1024]{1,0:T(8,128)} async-done(((f32[320,1024]{1,0:T(8,128)}), f32[320,1024]{1,0:T(8,128)}) %all-reduce.8.cloned.1.call-update) | async-done | bytes 1310736 | tf_op jit(solution)/shard_map/psum | solution.py:85
  451.2 21.0 %all-reduce.10.cloned.1.call-done = f32[320,1024]{1,0:T(8,128)} async-done(((f32[320,1024]{1,0:T(8,128)}), f32[320,1024]{1,0:T(8,128)}) %all-reduce.10.cloned.1.call-update) | async-done | bytes 1310736 | tf_op jit(solution)/shard_map/psum | solution.py:89
  481.2 6.8 all-to-all-start
  488.0 12.8 all-reduce.12.cloned.1.call-done
  502.3 239.7 %while.26 = (s32[]{:T(128)}, f32[1024,1024]{1,0:T(8,128)}, f32[1024]{0:T(1024)S(1)}, bf16[10,800,1024]{2,1,0:T(8,128)(2,1)}, bf16[10,800,1024]{2,1,0:T(8,128)(2,...) while((s32[]{:T(128)}, f32[1024,1024]{1,0:T(8,128)}, ...), condition=%wide.region_11.12_spmd.clone, body=%wide.region_9.11_spmd.clone.sunk | while | flops 5041816576 | bytes 50894132 | solution.py:134
  509.4 5.2 convert_reduce_fusion.3
  518.9 6.3 select_add_fusion.4
  532.2 5.2 convert_reduce_fusion.3
  541.6 7.6 select_add_fusion.4
  556.2 5.2 convert_reduce_fusion.3
  565.7 7.6 select_add_fusion.4
  580.3 5.2 convert_reduce_fusion.3
  589.9 7.6 select_add_fusion.4
  604.5 5.2 convert_reduce_fusion.3
  613.9 7.6 select_add_fusion.4
  628.5 5.2 convert_reduce_fusion.3
  638.1 7.6 select_add_fusion.4
  652.7 5.2 convert_reduce_fusion.3
  662.1 7.6 select_add_fusion.4
  676.7 5.2 convert_reduce_fusion.3
  686.3 7.6 select_add_fusion.4
  700.9 5.2 convert_reduce_fusion.3
  710.3 7.6 select_add_fusion.4
  724.9 5.2 convert_reduce_fusion.3
  734.4 7.6 select_add_fusion.4
  742.0 15.5 %copy.43 = bf16[500,16,1024]{2,0,1:T(8,128)(2,1)} copy(bf16[500,16,1024]{2,1,0:T(8,128)(2,1)} %bitcast.14) | data formatting | bytes 32768000 | tf_op jit(solution)/shard_map/reshape | solution.py:137
  757.5 6.8 all-to-all-start.1
  767.8 592.5 %all-reduce.16.cloned.1.call-done = (f32[1024,1024]{1,0:T(8,128)}, f32[1024,1024]{1,0:T(8,128)}) async-done(((f32[1024,1024]{1,0:T(8,128)}, f32[1024,1024]{1,0:T(8,128)}), (f32[1024,1024]{1,0:T(8,128)}, f32[1024,1024]{1,0:T(8,128)})) %all-reduce.16.cloned.1.call-update) | async-done | bytes 8388624 | tf_op jit(solution)/shard_map/psum | solution.py:151
  1360.8 14.9 %reshape.78 = bf16[8000,1024]{1,0:T(8,128)(2,1)} reshape(bf16[16,500,1024]{2,1,0:T(8,128)(2,1)} %all-to-all-done.1) | data formatting | bytes 32768000 | tf_op jit(solution)/shard_map/reshape | solution.py:144
  1375.8 10.4 fusion.13
  1386.2 41.3 %all-reduce = (f32[1024]{0:T(1024)S(1)}, f32[1024]{0:T(1024)}) all-reduce(f32[1024]{0:T(1024)S(1)} %get-tuple-element.90, f32[1024]{0:T(1024)S(1)} %get-tuple-element.157), channel_id=1, replica_groups=mesh['nodes'=16,'stream'=2] {'nodes'}, use_global_device_ids=true, to_apply=%region_15.16 | all-reduce | flops 2048 | bytes 16384 | tf_op jit(solution)/shard_map/psum | solution.py:151
  1430.5 4.9 copy.88
  (251 shorter events, 251.3 us)
Async XLA Ops:
  7.2 441.8 %copy-start = (bf16[1024,1024]{1,0:T(8,128)(2,1)S(1)}, bf16[1024,1024]{1,0:T(8,128)(2,1)}, u32[]{:S(2)}) copy-start(bf16[1024,1024]{1,0:T(8,128)(2,1)} %param.19) | copy-start | bytes 6291460
  7.2 440.2 %all-reduce.8.cloned.1.call-start = ((), (), s32[]{:S(2)}) async-start(), calls=%async_computation.3 | async-start | bytes 2621440 | tf_op jit(solution)/shard_map/psum | solution.py:85
  7.2 31.3 %collective-permute-start = (bf16[320,1024]{1,0:T(8,128)(2,1)}, bf16[320,1024]{1,0:T(8,128)(2,1)S(1)}, u32[]{:S(2)}, u32[]{:S(2)}) collective-permute-start(bf16[320,1024]{1,0:T(8,128)(2,1)} %param.13), channel_id=1, source_target_pairs={{0,2},{2,4},{4,6},{6,8},{8,10},{10,12},{12,14},{14,16},{16,18},{18... | collective-permute-start | bytes 1966088 | tf_op jit(solution)/shard_map/ppermute | solution.py:22
  10.2 30.7 %collective-permute-start.1 = (bf16[320,1024]{1,0:T(8,128)(2,1)}, bf16[320,1024]{1,0:T(8,128)(2,1)S(1)}, u32[]{:S(2)}, u32[]{:S(2)}) collective-permute-start(bf16[320,1024]{1,0:T(8,128)(2,1)} %param.13), channel_id=1, source_target_pairs={{0,30},{2,0},{4,2},{6,4},{8,6},{10,8},{12,10},{14,12},{16,14},{18,... | collective-permute-start | bytes 1966088 | tf_op jit(solution)/shard_map/ppermute | solution.py:27
  38.6 5.6 copy-start.12
  38.6 29.5 %collective-permute-start.2 = (bf16[320,1024]{1,0:T(8,128)(2,1)S(1)}, bf16[320,1024]{1,0:T(8,128)(2,1)S(1)}, u32[]{:S(2)}, u32[]{:S(2)}) collective-permute-start(bf16[320,1024]{1,0:T(8,128)(2,1)S(1)} %collective-permute-done), channel_id=1, source_target_pairs={{0,2},{2,4},{4,6},{6,8},{8,10},{10,12},{12,14},{14,16},{16,18},{18... | collective-permute-start | bytes 1966088 | tf_op jit(solution)/shard_map/ppermute | solution.py:22
  41.0 58.4 %copy-start.8 = (bf16[320,1024]{1,0:T(8,128)(2,1)}, bf16[320,1024]{1,0:T(8,128)(2,1)S(1)}, u32[]{:S(2)}) copy-start(bf16[320,1024]{1,0:T(8,128)(2,1)S(1)} %collective-permute-done.1) | copy-start | bytes 1966084
  41.0 29.6 %collective-permute-start.3 = (bf16[320,1024]{1,0:T(8,128)(2,1)S(1)}, bf16[320,1024]{1,0:T(8,128)(2,1)S(1)}, u32[]{:S(2)}, u32[]{:S(2)}) collective-permute-start(bf16[320,1024]{1,0:T(8,128)(2,1)S(1)} %collective-permute-done.1), channel_id=1, source_target_pairs={{0,30},{2,0},{4,2},{6,4},{8,6},{10,8},{12,10},{14,12},{16,14},{18,... | collective-permute-start | bytes 1966088 | tf_op jit(solution)/shard_map/ppermute | solution.py:27
  68.1 28.7 %collective-permute-start.4 = (bf16[320,1024]{1,0:T(8,128)(2,1)S(1)}, bf16[320,1024]{1,0:T(8,128)(2,1)S(1)}, u32[]{:S(2)}, u32[]{:S(2)}) collective-permute-start(bf16[320,1024]{1,0:T(8,128)(2,1)S(1)} %collective-permute-done.2), channel_id=1, source_target_pairs={{0,2},{2,4},{4,6},{6,8},{8,10},{10,12},{12,14},{14,16},{16,18},{18... | collective-permute-start | bytes 1966088 | tf_op jit(solution)/shard_map/ppermute | solution.py:22
  70.6 26.2 %copy-start.6 = (bf16[320,1024]{1,0:T(8,128)(2,1)}, bf16[320,1024]{1,0:T(8,128)(2,1)S(1)}, u32[]{:S(2)}) copy-start(bf16[320,1024]{1,0:T(8,128)(2,1)S(1)} %collective-permute-done.3) | copy-start | bytes 1966084
  70.6 28.7 %collective-permute-start.5 = (bf16[320,1024]{1,0:T(8,128)(2,1)S(1)}, bf16[320,1024]{1,0:T(8,128)(2,1)}, u32[]{:S(2)}, u32[]{:S(2)}) collective-permute-start(bf16[320,1024]{1,0:T(8,128)(2,1)S(1)} %collective-permute-done.3), channel_id=1, source_target_pairs={{0,30},{2,0},{4,2},{6,4},{8,6},{10,8},{12,10},{14,12},{16,14},{18,... | collective-permute-start | bytes 1966088 | tf_op jit(solution)/shard_map/ppermute | solution.py:27
  96.8 18.5 %copy-start.10 = (bf16[320,1024]{1,0:T(8,128)(2,1)}, bf16[320,1024]{1,0:T(8,128)(2,1)S(1)}, u32[]{:S(2)}) copy-start(bf16[320,1024]{1,0:T(8,128)(2,1)S(1)} %collective-permute-done.4) | copy-start | bytes 1966084
  96.8 28.7 %collective-permute-start.6 = (bf16[320,1024]{1,0:T(8,128)(2,1)S(1)}, bf16[320,1024]{1,0:T(8,128)(2,1)}, u32[]{:S(2)}, u32[]{:S(2)}) collective-permute-start(bf16[320,1024]{1,0:T(8,128)(2,1)S(1)} %collective-permute-done.4), channel_id=1, source_target_pairs={{0,2},{2,4},{4,6},{6,8},{8,10},{10,12},{12,14},{14,16},{16,18},{18... | collective-permute-start | bytes 1966088 | tf_op jit(solution)/shard_map/ppermute | solution.py:22
  99.3 29.9 %collective-permute-start.7 = (bf16[320,1024]{1,0:T(8,128)(2,1)}, bf16[320,1024]{1,0:T(8,128)(2,1)}, u32[]{:S(2)}, u32[]{:S(2)}) collective-permute-start(bf16[320,1024]{1,0:T(8,128)(2,1)} %collective-permute-done.5), channel_id=1, source_target_pairs={{0,30},{2,0},{4,2},{6,4},{8,6},{10,8},{12,10},{14,12},{16,14},{18,... | collective-permute-start | bytes 1966088 | tf_op jit(solution)/shard_map/ppermute | solution.py:27
  125.5 34.9 %collective-permute-start.8 = (bf16[320,1024]{1,0:T(8,128)(2,1)}, bf16[320,1024]{1,0:T(8,128)(2,1)}, u32[]{:S(2)}, u32[]{:S(2)}) collective-permute-start(bf16[320,1024]{1,0:T(8,128)(2,1)} %collective-permute-done.6), channel_id=1, source_target_pairs={{0,2},{2,4},{4,6},{6,8},{8,10},{10,12},{12,14},{14,16},{16,18},{18... | collective-permute-start | bytes 1966088 | tf_op jit(solution)/shard_map/ppermute | solution.py:22
  129.3 44.8 %collective-permute-start.9 = (bf16[320,1024]{1,0:T(8,128)(2,1)}, bf16[320,1024]{1,0:T(8,128)(2,1)}, u32[]{:S(2)}, u32[]{:S(2)}) collective-permute-start(bf16[320,1024]{1,0:T(8,128)(2,1)} %collective-permute-done.7), channel_id=1, source_target_pairs={{0,30},{2,0},{4,2},{6,4},{8,6},{10,8},{12,10},{14,12},{16,14},{18,... | collective-permute-start | bytes 1966088 | tf_op jit(solution)/shard_map/ppermute | solution.py:27
  160.4 31.1 %collective-permute-start.10 = (bf16[320,1024]{1,0:T(8,128)(2,1)}, bf16[320,1024]{1,0:T(8,128)(2,1)}, u32[]{:S(2)}, u32[]{:S(2)}) collective-permute-start(bf16[320,1024]{1,0:T(8,128)(2,1)} %collective-permute-done.8), channel_id=1, source_target_pairs={{0,2},{2,4},{4,6},{6,8},{8,10},{10,12},{12,14},{14,16},{16,18},{18... | collective-permute-start | bytes 1966088 | tf_op jit(solution)/shard_map/ppermute | solution.py:22
  162.9 5.3 copy-start.3
  162.9 6.2 copy-start.13
  162.9 27.7 %copy-start.9 = (bf16[320,1024]{1,0:T(8,128)(2,1)S(1)}, bf16[320,1024]{1,0:T(8,128)(2,1)}, u32[]{:S(2)}) copy-start(bf16[320,1024]{1,0:T(8,128)(2,1)} %copy-done.8) | copy-start | bytes 1966084
  168.3 24.1 %copy-start.7 = (bf16[320,1024]{1,0:T(8,128)(2,1)S(1)}, bf16[320,1024]{1,0:T(8,128)(2,1)}, u32[]{:S(2)}) copy-start(bf16[320,1024]{1,0:T(8,128)(2,1)} %copy-done.6) | copy-start | bytes 1966084
  168.3 25.1 %copy-start.11 = (bf16[320,1024]{1,0:T(8,128)(2,1)S(1)}, bf16[320,1024]{1,0:T(8,128)(2,1)}, u32[]{:S(2)}) copy-start(bf16[320,1024]{1,0:T(8,128)(2,1)} %copy-done.10) | copy-start | bytes 1966084
  174.1 29.3 %collective-permute-start.11 = (bf16[320,1024]{1,0:T(8,128)(2,1)}, bf16[320,1024]{1,0:T(8,128)(2,1)S(1)}, u32[]{:S(2)}, u32[]{:S(2)}) collective-permute-start(bf16[320,1024]{1,0:T(8,128)(2,1)} %collective-permute-done.9), channel_id=1, source_target_pairs={{0,30},{2,0},{4,2},{6,4},{8,6},{10,8},{12,10},{14,12},{16,14},{18,... | collective-permute-start | bytes 1966088 | tf_op jit(solution)/shard_map/ppermute | solution.py:27
  191.5 30.3 %collective-permute-start.12 = (bf16[320,1024]{1,0:T(8,128)(2,1)}, bf16[320,1024]{1,0:T(8,128)(2,1)S(1)}, u32[]{:S(2)}, u32[]{:S(2)}) collective-permute-start(bf16[320,1024]{1,0:T(8,128)(2,1)} %collective-permute-done.10), channel_id=1, source_target_pairs={{0,2},{2,4},{4,6},{6,8},{8,10},{10,12},{12,14},{14,16},{16,18},{18... | collective-permute-start | bytes 1966088 | tf_op jit(solution)/shard_map/ppermute | solution.py:22
  203.3 28.0 %collective-permute-start.13 = (bf16[320,1024]{1,0:T(8,128)(2,1)S(1)}, bf16[320,1024]{1,0:T(8,128)(2,1)S(1)}, u32[]{:S(2)}, u32[]{:S(2)}) collective-permute-start(bf16[320,1024]{1,0:T(8,128)(2,1)S(1)} %collective-permute-done.11), channel_id=1, source_target_pairs={{0,30},{2,0},{4,2},{6,4},{8,6},{10,8},{12,10},{14,12},{16,14},{18,... | collective-permute-start | bytes 1966088 | tf_op jit(solution)/shard_map/ppermute | solution.py:27
  221.8 17.3 %collective-permute-start.14 = (bf16[320,1024]{1,0:T(8,128)(2,1)S(1)}, bf16[320,1024]{1,0:T(8,128)(2,1)S(1)}, u32[]{:S(2)}, u32[]{:S(2)}) collective-permute-start(bf16[320,1024]{1,0:T(8,128)(2,1)S(1)} %collective-permute-done.12), channel_id=1, source_target_pairs={{0,2},{2,4},{4,6},{6,8},{8,10},{10,12},{12,14},{14,16},{16,18},{18... | collective-permute-start | bytes 1966088 | tf_op jit(solution)/shard_map/ppermute | solution.py:22
  256.3 15.5 %copy-start.16 = (f32[1024]{0:T(1024)S(1)}, f32[1024]{0:T(1024)}, u32[]{:S(2)}) copy-start(f32[1024]{0:T(1024)} %param.18) | copy-start | bytes 12292
  422.0 50.3 %all-reduce.10.cloned.1.call-start = ((), (), s32[]{:S(2)}) async-start(), calls=%async_computation.4 | async-start | bytes 2621440 | tf_op jit(solution)/shard_map/psum | solution.py:89
  449.0 23.3 %copy-start.4 = (bf16[320,1024]{1,0:T(8,128)(2,1)S(1)}, bf16[320,1024]{1,0:T(8,128)(2,1)}, u32[]{:S(2)}) copy-start(bf16[320,1024]{1,0:T(8,128)(2,1)} %param.21) | copy-start | bytes 1966084
  449.0 23.3 %copy-start.14 = (f32[1024]{0:T(1024)S(1)}, f32[1024]{0:T(1024)}, u32[]{:S(2)}) copy-start(f32[1024]{0:T(1024)} %param.20) | copy-start | bytes 12292
  451.0 49.9 %all-reduce.12.cloned.1.call-start = ((), (), s32[]{:S(2)}) async-start(), calls=%async_computation.5 | async-start | bytes 2621440 | tf_op jit(solution)/shard_map/psum | solution.py:36
  481.2 276.3 %all-to-all-start = ((s32[16,1,500]{2,1,0:T(1,128)}), s32[16,1,500]{2,1,0:T(1,128)S(1)}, u32[]{:S(2)}, u32[]{:S(2)}) async-start(s32[16,1,500]{2,1,0:T(1,128)} %copy.37), calls=%async_computation | async-start | bytes 65536 | tf_op jit(solution)/shard_map/all_to_all | solution.py:139
  509.4 6.4 copy-start.15
  514.6 1.2 copy-start.17
  532.2 6.4 copy-start.15
  537.4 1.2 copy-start.17
  556.2 6.4 copy-start.15
  561.5 1.2 copy-start.17
  580.3 6.4 copy-start.15
  585.5 1.2 copy-start.17
  604.4 6.4 copy-start.15
  609.7 1.2 copy-start.17
  628.5 6.4 copy-start.15
  633.8 1.2 copy-start.17
  652.6 6.4 copy-start.15
  657.9 1.2 copy-start.17
  676.7 6.4 copy-start.15
  681.9 1.2 copy-start.17
  700.9 6.4 copy-start.15
  706.1 1.2 copy-start.17
  724.9 6.4 copy-start.15
  730.1 1.2 copy-start.17
  757.5 603.3 %all-to-all-start.1 = ((bf16[16,500,1024]{2,1,0:T(8,128)(2,1)}), bf16[16,500,1024]{2,1,0:T(8,128)(2,1)}, u32[]{:S(2)}, u32[]{:S(2)}) async-start(bf16[16,500,1024]{2,1,0:T(8,128)(2,1)} %bitcast.80), calls=%async_computation.1 | async-start | bytes 33030144 | tf_op jit(solution)/shard_map/all_to_all | solution.py:140
  764.4 595.9 %all-reduce.16.cloned.1.call-start = ((), (), s32[]{:S(2)}) async-start(), calls=%async_computation.8 | async-start | bytes 16777216 | tf_op jit(solution)/shard_map/psum | solution.py:151
  767.8 662.8 %all-reduce.14.cloned.1.call-start = ((), (), s32[]{:S(2)}) async-start(), calls=%async_computation.7 | async-start | bytes 8388608 | tf_op jit(solution)/shard_map/psum | solution.py:154
  1360.3 70.2 %reduce-scatter.2.cloned.1.call-start = ((), (), s32[]{:S(2)}) async-start(), calls=%async_computation.6 | async-start | bytes 1966080 | tf_op jit(solution)/shard_map/reduce_scatter | solution.py:148
  1360.8 15.0 %copy-start.5 = (f32[320,1024]{1,0:T(8,128)S(1)}, f32[320,1024]{1,0:T(8,128)}, u32[]{:S(2)}) copy-start(f32[320,1024]{1,0:T(8,128)} %get-tuple-element.169) | copy-start | bytes 3932164
  1430.5 4.9 copy-start.2
  1430.5 7.0 copy-start.1
Sparse Core Ops, SparseCore 0:
  422.1 25.1 all-reduce.7
  451.1 21.1 all-reduce.9
  479.7 21.1 all-reduce.11
  772.8 587.4 all-reduce.15
  1362.8 27.3 all-reduce.13
  1392.9 9.9 reduce-scatter.1
